TPU v7x, 128 devices: a whole 4x4x4 slice. The times are simulated.
128 devices in a mesh: segment: 4 (over z), expert: 8 (over y, core), tensor: 4 (over x).
Axes of the slice: x: 4, y: 4, z: 4, core: 2. Of those that a mesh axis runs over, the one named last changes fastest.
Arguments:
- inputs: bfloat16 [2, 512, 3072], P(None, 'expert', 'tensor'), may hold values from -40 to 40
- norm_gain: float32 [4, 3072], P('segment', 'tensor'), may hold values from 0.5 to 1.5
- up_weight: bfloat16 [4, 8, 3072, 8192], P('segment', 'expert', None, 'tensor'), may hold values from -0.109375 to 0.109375
- down_weight: bfloat16 [4, 8, 8192, 3072], P('segment', 'expert', 'tensor'), may hold values from -0.0625 to 0.0625
- routing: int32 [4, 2, 512, 2], P('segment', None, 'expert'), may hold values from 0 to 7, all different within a row; in each aligned block of 64 rows (0 to 63, 64 to 127, ..., all dimensions but the last counted through in order) at most 32 rows name the same one
- gates: float32 [4, 2, 512, 2], P('segment', None, 'expert'), may hold values from 0.2 to 1
Outputs:
- segment_out: bfloat16 [4, 2, 512, 3072], P('segment', None, 'expert', 'tensor')
Inputs may be any that keep to these rules, and one draw needn't show every extreme that they name: `routing`: in each aligned block of 64 rows of one segment and micro-batch (the rows of one index of the expert axis) no expert is named by more than 32 rows, a bound that some block reaches; the 2 experts of a row differ.
All inputs are finite; a program needn't handle non-finite values.
Results may differ from a plain program's by a relative error of at most 0.013.
Values may be sent and summed in bfloat16 or wider, within the bound.
A program may use at most 128 MiB of HBM per device.

v0:
```python
import jax
import jax.numpy as jnp
from jax import lax
from jax.sharding import PartitionSpec as P


def passed_along(value, axis, steps):
    count = lax.axis_size(axis)
    initial, last = (max(0, -steps), min(count, count - steps))
    return lax.ppermute(value, axis, [(source, source + steps) for source in range(initial, last)])


def slot_numbers(choices, expert_count):
    flat_ids = choices.reshape(-1)
    onehot = (flat_ids[:, None] == jnp.arange(expert_count, dtype=jnp.int32)[None, :]).astype(
        jnp.int32
    )
    earlier = jnp.cumsum(onehot, axis=0) - onehot
    return jnp.sum(earlier * onehot, axis=1)


def on_device(inputs, norm_gain, up_weight, down_weight, routing, gates):
    segment_count = lax.axis_size("segment")
    expert_count = lax.axis_size("expert")
    tensor_count = lax.axis_size("tensor")
    segment_index = lax.axis_index("segment")
    batches = inputs.shape[0]
    row_count = inputs.shape[1]
    quarter = inputs.shape[2]
    width = quarter * tensor_count
    capacity = min(row_count, 4 * row_count // expert_count)
    slot_total = expert_count * capacity
    up_local = up_weight[0, 0]
    down_local = down_weight[0, 0]
    hidden_local = up_local.shape[1]
    gain_row = norm_gain[0]
    targets_all = jnp.arange(slot_total, dtype=jnp.int32)
    received = jnp.zeros((row_count, quarter), jnp.bfloat16)
    stored = jnp.zeros((batches, row_count, quarter), jnp.bfloat16)
    tick_count = batches + segment_count - 1
    batch_ids = jnp.arange(batches, dtype=jnp.int32)
    for tick_index in range(tick_count):
        batch_now = tick_index - segment_index
        active = (batch_now >= 0) & (batch_now < batches)
        batch_safe = jnp.clip(batch_now, 0, batches - 1)
        first_input = inputs[min(tick_index, batches - 1)]
        stream = jnp.where(segment_index == 0, first_input, received)
        stream_f = stream.astype(jnp.float32)
        squares = lax.psum(jnp.sum(stream_f * stream_f, axis=1), "tensor")
        normed = (stream_f * lax.rsqrt(squares[:, None] / width + 1e-05) * gain_row).astype(
            jnp.bfloat16
        )
        choices = lax.dynamic_index_in_dim(routing[0], batch_safe, 0, keepdims=False)
        weights = lax.dynamic_index_in_dim(gates[0], batch_safe, 0, keepdims=False)
        slot_ids = slot_numbers(choices, expert_count).reshape(row_count, choices.shape[1])
        target = choices * capacity + slot_ids
        placed = (target[:, :, None] == targets_all[None, None, :]).astype(jnp.float32)
        dispatch_mat = jnp.sum(placed, axis=1).astype(jnp.bfloat16)
        combine_mat = jnp.sum(placed * weights[:, :, None], axis=1)
        outgoing = jnp.einsum("rs,rd->sd", dispatch_mat, normed, preferred_element_type=jnp.float32)
        outgoing = outgoing.astype(jnp.bfloat16).reshape(expert_count, capacity, quarter)
        copies = jnp.broadcast_to(
            outgoing[:, None], (expert_count, tensor_count, capacity, quarter)
        )
        copies = copies.reshape(expert_count * tensor_count, capacity, quarter)
        arrived = lax.all_to_all(
            copies, ("expert", "tensor"), split_axis=0, concat_axis=0, tiled=True
        )
        full_rows = (
            arrived.reshape(expert_count, tensor_count, capacity, quarter)
            .transpose(0, 2, 1, 3)
            .reshape(slot_total, width)
        )

        def expert_work(rows_in):
            hidden = jax.nn.silu(
                jnp.dot(rows_in, up_local, preferred_element_type=jnp.float32)
            ).astype(jnp.bfloat16)
            return jnp.einsum(
                "ecf,ftd->etcd",
                hidden.reshape(expert_count, capacity, hidden_local),
                down_local.reshape(hidden_local, tensor_count, quarter),
                preferred_element_type=jnp.float32,
            ).astype(jnp.bfloat16)

        def spare_work(rows_in):
            return jnp.zeros((expert_count, tensor_count, capacity, quarter), jnp.bfloat16)

        partials = lax.cond(active, expert_work, spare_work, full_rows)
        partials = partials.reshape(expert_count * tensor_count, capacity, quarter)
        returned = lax.all_to_all(
            partials, ("expert", "tensor"), split_axis=0, concat_axis=0, tiled=True
        )
        returned_f = returned.astype(jnp.float32).reshape(
            expert_count, tensor_count, capacity, quarter
        )
        expert_out = jnp.sum(returned_f, axis=1).reshape(slot_total, quarter)
        updated = stream_f + jnp.dot(combine_mat, expert_out, precision=lax.Precision.HIGHEST)
        result = updated.astype(jnp.bfloat16)
        keep_mask = (batch_ids == batch_now) & active
        stored = jnp.where(keep_mask[:, None, None], result[None], stored)
        if tick_index + 1 < tick_count:
            received = passed_along(result, "segment", 1)
    return stored[None]


def solution(mesh):
    return jax.shard_map(
        on_device,
        mesh=mesh,
        in_specs=(
            P(None, "expert", "tensor"),
            P("segment", "tensor"),
            P("segment", "expert", None, "tensor"),
            P("segment", "expert", "tensor", None),
            P("segment", None, "expert", None),
            P("segment", None, "expert", None),
        ),
        out_specs=P("segment", None, "expert", "tensor"),
        check_vma=False,
    )
```

profile of v0, /device:TPU:97, one launch (start us, length us, event | category | flops | bytes accessed | tf_op | source)
XLA Modules:
  0.0 566.9 jit_solution(17162160675324440377)
XLA Ops:
  1.7 1.4 fusion.92
  4.2 8.5 %psum.35 = f32[64]{0:T(128)S(1)} all-reduce(f32[64]{0:T(128)S(1)} %fusion.62), channel_id=1, replica_groups=mesh['segment'=4,'expert'=8,'tensor'=4] {'tensor'}, use_global_device_ids=true, to_apply=%region_5.6 | all-reduce | flops 64 | bytes 512 | tf_op jit(solution)/shard_map/psum | solution.py:49
  14.7 1.3 broadcast_in_dim.136
  16.1 7.6 %all-to-all-start = ((bf16[32,32,768]{2,1,0:T(8,128)(2,1)}), bf16[32,32,768]{2,1,0:T(8,128)(2,1)S(1)}, u32[]{:S(2)}, u32[]{:S(2)}) async-start(bf16[32,32,768]{2,1,0:T(8,128)(2,1)} %bitcast.31), calls=%async_computation | async-start | bytes 3145728 | tf_op jit(solution)/shard_map/all_to_all | solution.py:66
  23.7 21.4 %all-to-all-done = bf16[32,32,768]{2,1,0:T(8,128)(2,1)S(1)} async-done(((bf16[32,32,768]{2,1,0:T(8,128)(2,1)}), bf16[32,32,768]{2,1,0:T(8,128)(2,1)S(1)}, u32[]{:S(2)}, u32[]{:S(2)}) %all-to-all-start) | async-done | bytes 1572896 | tf_op jit(solution)/shard_map/all_to_all | solution.py:66
  45.1 1.4 conditional.5
  45.1 1.4 broadcast.206
  46.5 5.5 all-to-all-start.1
  54.4 19.0 %all-to-all-done.1 = bf16[32,32,768]{2,1,0:T(8,128)(2,1)S(1)} async-done(((bf16[32,32,768]{2,1,0:T(8,128)(2,1)}), bf16[32,32,768]{2,1,0:T(8,128)(2,1)S(1)}, u32[]{:S(2)}, u32[]{:S(2)}) %all-to-all-start.1) | async-done | bytes 1572896 | tf_op jit(solution)/shard_map/all_to_all | solution.py:91
  74.2 1.3 collective-permute-start
  76.2 3.3 collective-permute-done
  79.7 9.3 %psum.36 = f32[64]{0:T(128)S(1)} all-reduce(f32[64]{0:T(128)S(1)} %get-tuple-element.116), channel_id=1, replica_groups=mesh['segment'=4,'expert'=8,'tensor'=4] {'tensor'}, use_global_device_ids=true, to_apply=%region_14.15 | all-reduce | flops 64 | bytes 512 | tf_op jit(solution)/shard_map/psum | solution.py:49
  89.3 1.3 broadcast_in_dim.138
  90.6 6.4 %all-to-all-start.2 = ((bf16[32,32,768]{2,1,0:T(8,128)(2,1)}), bf16[32,32,768]{2,1,0:T(8,128)(2,1)S(1)}, u32[]{:S(2)}, u32[]{:S(2)}) async-start(bf16[32,32,768]{2,1,0:T(8,128)(2,1)} %bitcast.41), calls=%async_computation.2 | async-start | bytes 3145728 | tf_op jit(solution)/shard_map/all_to_all | solution.py:66
  97.0 21.4 %all-to-all-done.2 = bf16[32,32,768]{2,1,0:T(8,128)(2,1)S(1)} async-done(((bf16[32,32,768]{2,1,0:T(8,128)(2,1)}), bf16[32,32,768]{2,1,0:T(8,128)(2,1)S(1)}, u32[]{:S(2)}, u32[]{:S(2)}) %all-to-all-start.2) | async-done | bytes 1572896 | tf_op jit(solution)/shard_map/all_to_all | solution.py:66
  118.7 28.1 %all_to_all.50 = bf16[32,32,768]{2,1,0:T(8,128)(2,1)S(1)} all-to-all(bf16[32,32,768]{2,1,0:T(8,128)(2,1)S(1)} %bitcast.228), channel_id=1, replica_groups=mesh['segment'=4,'expert'=8,'tensor'=4] {'expert','tensor'}, dimensions={0} | all-to-all | bytes 3145728 | tf_op jit(solution)/shard_map/all_to_all | solution.py:91
  147.6 1.3 collective-permute-start.1
  149.1 4.3 collective-permute-done.1
  153.5 7.2 %psum.37 = f32[64]{0:T(128)S(1)} all-reduce(f32[64]{0:T(128)S(1)} %get-tuple-element.114), channel_id=1, replica_groups=mesh['segment'=4,'expert'=8,'tensor'=4] {'tensor'}, use_global_device_ids=true, to_apply=%region_23.24 | all-reduce | flops 64 | bytes 512 | tf_op jit(solution)/shard_map/psum | solution.py:49
  161.0 1.3 broadcast_in_dim.140
  162.4 7.0 %all-to-all-start.4 = ((bf16[32,32,768]{2,1,0:T(8,128)(2,1)}), bf16[32,32,768]{2,1,0:T(8,128)(2,1)S(1)}, u32[]{:S(2)}, u32[]{:S(2)}) async-start(bf16[32,32,768]{2,1,0:T(8,128)(2,1)} %bitcast.50), calls=%async_computation.4 | async-start | bytes 3145728 | tf_op jit(solution)/shard_map/all_to_all | solution.py:66
  169.4 21.4 %all-to-all-done.4 = bf16[32,32,768]{2,1,0:T(8,128)(2,1)S(1)} async-done(((bf16[32,32,768]{2,1,0:T(8,128)(2,1)}), bf16[32,32,768]{2,1,0:T(8,128)(2,1)S(1)}, u32[]{:S(2)}, u32[]{:S(2)}) %all-to-all-start.4) | async-done | bytes 1572896 | tf_op jit(solution)/shard_map/all_to_all | solution.py:66
  190.8 1.6 conditional.7
  190.8 1.4 broadcast.208
  192.4 5.6 all-to-all-start.5
  200.4 19.0 %all-to-all-done.5 = bf16[32,32,768]{2,1,0:T(8,128)(2,1)S(1)} async-done(((bf16[32,32,768]{2,1,0:T(8,128)(2,1)}), bf16[32,32,768]{2,1,0:T(8,128)(2,1)S(1)}, u32[]{:S(2)}, u32[]{:S(2)}) %all-to-all-start.5) | async-done | bytes 1572896 | tf_op jit(solution)/shard_map/all_to_all | solution.py:91
  220.2 1.3 collective-permute-start.2
  222.2 121.0 %collective-permute-done.2 = bf16[64,768]{1,0:T(8,128)(2,1)S(1)} collective-permute-done((bf16[64,768]{1,0:T(8,128)(2,1)S(1)}, bf16[64,768]{1,0:T(8,128)(2,1)S(1)}, u32[]{:S(2)}, u32[]{:S(2)}) %collective-permute-start.2) | collective-permute-done | bytes 98336 | tf_op jit(solution)/shard_map/ppermute | solution.py:10
  343.3 9.4 %psum.38 = f32[64]{0:T(128)S(1)} all-reduce(f32[64]{0:T(128)S(1)} %get-tuple-element.112), channel_id=1, replica_groups=mesh['segment'=4,'expert'=8,'tensor'=4] {'tensor'}, use_global_device_ids=true, to_apply=%region_32.33 | all-reduce | flops 64 | bytes 512 | tf_op jit(solution)/shard_map/psum | solution.py:49
  353.0 1.3 broadcast_in_dim.142
  354.4 6.1 %all-to-all-start.6 = ((bf16[32,32,768]{2,1,0:T(8,128)(2,1)}), bf16[32,32,768]{2,1,0:T(8,128)(2,1)S(1)}, u32[]{:S(2)}, u32[]{:S(2)}) async-start(bf16[32,32,768]{2,1,0:T(8,128)(2,1)} %bitcast.59), calls=%async_computation.6 | async-start | bytes 3145728 | tf_op jit(solution)/shard_map/all_to_all | solution.py:66
  360.5 21.4 %all-to-all-done.6 = bf16[32,32,768]{2,1,0:T(8,128)(2,1)S(1)} async-done(((bf16[32,32,768]{2,1,0:T(8,128)(2,1)}), bf16[32,32,768]{2,1,0:T(8,128)(2,1)S(1)}, u32[]{:S(2)}, u32[]{:S(2)}) %all-to-all-start.6) | async-done | bytes 1572896 | tf_op jit(solution)/shard_map/all_to_all | solution.py:66
  381.9 41.5 %conditional.8 = (bf16[8,4,32,768]{3,2,1,0:T(8,128)(2,1)S(1)}) conditional(s32[]{:T(128)} %convert_element_type.200, () %tuple.41, (bf16[8,32,4,768]{3,1,2,0:T(8,128)(2,1)S(1)}, bf16[3072,2048]{1,0:T(8,128)(2,1)}, bf16[1,1,2048,3072]{3,2,1,0:T(8,128)(2,1)}) %tuple.94), branch_computations={%region_33.34_spmd, %region_34.35_spmd} | conditional | flops 6445858816 | bytes 61865992 | solution.py:89
  383.8 8.1 %multiply_convert_fusion.3 = bf16[256,2048]{1,0:T(8,128)(2,1)S(1)} fusion(bf16[256,3072]{1,0:T(8,128)(2,1)S(1)} %bitcast.243, bf16[3072,2048]{1,0:T(8,128)(2,1)} %get-tuple-element.65), kind=kOutput, calls=%fused_computation.21 | convolution fusion | flops 3223846912 | bytes 15204352 | tf_op jit(solution)/shard_map/cond/branch_1_fun/dot_general | solution.py:77
  392.0 23.5 %reshape_squeeze.13 = bf16[2048,4,768]{2,1,0:T(4,128)(2,1)} reshape(bf16[1,1,2048,3072]{3,2,1,0:T(8,128)(2,1)} %get-tuple-element.66) | data formatting | bytes 25165824 | tf_op jit(solution)/shard_map/cond/branch_1_fun/reshape;squeeze | solution.py:82
  415.4 8.0 %fusion.33 = bf16[8,4,32,768]{3,2,1,0:T(8,128)(2,1)S(1)} fusion(bf16[8,32,2048,1]{2,1,3,0:T(8,128)(2,1)S(1)} %bitcast.258, bf16[2048,4,768]{2,1,0:T(4,128)(2,1)} %reshape_squeeze.13), kind=kOutput, calls=%fused_computation.23 | convolution fusion | flops 3222011904 | bytes 15204352 | tf_op jit(solution)/shard_map/cond/branch_1_fun/ecf,ftd->etcd/dot_general | solution.py:79
  423.4 28.1 %all_to_all.51 = bf16[32,32,768]{2,1,0:T(8,128)(2,1)S(1)} all-to-all(bf16[32,32,768]{2,1,0:T(8,128)(2,1)S(1)} %bitcast.229), channel_id=1, replica_groups=mesh['segment'=4,'expert'=8,'tensor'=4] {'expert','tensor'}, dimensions={0} | all-to-all | bytes 3145728 | tf_op jit(solution)/shard_map/all_to_all | solution.py:91
  453.8 4.3 collective-permute-done.3
  458.2 7.2 %psum.39 = f32[64]{0:T(128)S(1)} all-reduce(f32[64]{0:T(128)S(1)} %get-tuple-element.110), channel_id=1, replica_groups=mesh['segment'=4,'expert'=8,'tensor'=4] {'tensor'}, use_global_device_ids=true, to_apply=%region_41.42 | all-reduce | flops 64 | bytes 512 | tf_op jit(solution)/shard_map/psum | solution.py:49
  465.8 1.3 broadcast_in_dim.144
  467.1 7.0 %all-to-all-start.8 = ((bf16[32,32,768]{2,1,0:T(8,128)(2,1)}), bf16[32,32,768]{2,1,0:T(8,128)(2,1)S(1)}, u32[]{:S(2)}, u32[]{:S(2)}) async-start(bf16[32,32,768]{2,1,0:T(8,128)(2,1)} %bitcast.68), calls=%async_computation.8 | async-start | bytes 3145728 | tf_op jit(solution)/shard_map/all_to_all | solution.py:66
  474.1 21.4 %all-to-all-done.8 = bf16[32,32,768]{2,1,0:T(8,128)(2,1)S(1)} async-done(((bf16[32,32,768]{2,1,0:T(8,128)(2,1)}), bf16[32,32,768]{2,1,0:T(8,128)(2,1)S(1)}, u32[]{:S(2)}, u32[]{:S(2)}) %all-to-all-start.8) | async-done | bytes 1572896 | tf_op jit(solution)/shard_map/all_to_all | solution.py:66
  495.6 42.5 %conditional.9 = (bf16[8,4,32,768]{3,2,1,0:T(8,128)(2,1)}) conditional(s32[]{:T(128)} %convert_element_type.208, () %tuple.43, (bf16[8,32,4,768]{3,1,2,0:T(8,128)(2,1)S(1)}, bf16[3072,2048]{1,0:T(8,128)(2,1)}, bf16[1,1,2048,3072]{3,2,1,0:T(8,128)(2,1)}) %tuple.95), branch_computations={%region_42.43_spmd, %region_43.44_spmd} | conditional | flops 6445858816 | bytes 61865992 | solution.py:89
  497.2 8.1 %multiply_convert_fusion.4 = bf16[256,2048]{1,0:T(8,128)(2,1)S(1)} fusion(bf16[256,3072]{1,0:T(8,128)(2,1)S(1)} %bitcast.244, bf16[3072,2048]{1,0:T(8,128)(2,1)} %get-tuple-element.68), kind=kOutput, calls=%fused_computation.27 | convolution fusion | flops 3223846912 | bytes 15204352 | tf_op jit(solution)/shard_map/cond/branch_1_fun/dot_general | solution.py:77
  505.4 23.5 %reshape_squeeze.14 = bf16[2048,4,768]{2,1,0:T(4,128)(2,1)} reshape(bf16[1,1,2048,3072]{3,2,1,0:T(8,128)(2,1)} %get-tuple-element.69) | data formatting | bytes 25165824 | tf_op jit(solution)/shard_map/cond/branch_1_fun/reshape;squeeze | solution.py:82
  528.8 9.2 %fusion.42 = bf16[8,4,32,768]{3,2,1,0:T(8,128)(2,1)} fusion(bf16[8,32,2048,1]{2,1,3,0:T(8,128)(2,1)S(1)} %bitcast.259, bf16[2048,4,768]{2,1,0:T(4,128)(2,1)} %reshape_squeeze.14), kind=kOutput, calls=%fused_computation.29 | convolution fusion | flops 3222011904 | bytes 15204352 | tf_op jit(solution)/shard_map/cond/branch_1_fun/ecf,ftd->etcd/dot_general | solution.py:79
  538.1 5.6 all-to-all-start.9
  543.7 21.3 %all-to-all-done.9 = bf16[32,32,768]{2,1,0:T(8,128)(2,1)S(1)} async-done(((bf16[32,32,768]{2,1,0:T(8,128)(2,1)}), bf16[32,32,768]{2,1,0:T(8,128)(2,1)S(1)}, u32[]{:S(2)}, u32[]{:S(2)}) %all-to-all-start.9) | async-done | bytes 1572896 | tf_op jit(solution)/shard_map/all_to_all | solution.py:91
  (103 shorter events, 22.6 us)
Async XLA Ops:
  16.1 29.0 %all-to-all-start = ((bf16[32,32,768]{2,1,0:T(8,128)(2,1)}), bf16[32,32,768]{2,1,0:T(8,128)(2,1)S(1)}, u32[]{:S(2)}, u32[]{:S(2)}) async-start(bf16[32,32,768]{2,1,0:T(8,128)(2,1)} %bitcast.31), calls=%async_computation | async-start | bytes 3145728 | tf_op jit(solution)/shard_map/all_to_all | solution.py:66
  46.5 26.9 %all-to-all-start.1 = ((bf16[32,32,768]{2,1,0:T(8,128)(2,1)}), bf16[32,32,768]{2,1,0:T(8,128)(2,1)S(1)}, u32[]{:S(2)}, u32[]{:S(2)}) async-start(bf16[32,32,768]{2,1,0:T(8,128)(2,1)} %bitcast.35), calls=%async_computation.1 | async-start | bytes 3145728 | tf_op jit(solution)/shard_map/all_to_all | solution.py:91
  52.0 21.6 %copy-start = (bf16[2,64,768]{2,1,0:T(8,128)(2,1)S(1)}, bf16[2,64,768]{2,1,0:T(8,128)(2,1)}, u32[]{:S(2)}) copy-start(bf16[2,64,768]{2,1,0:T(8,128)(2,1)} %param.16) | copy-start | bytes 589828
  74.2 2.0 copy-start.3
  74.2 5.4 collective-permute-start
  90.6 27.8 %all-to-all-start.2 = ((bf16[32,32,768]{2,1,0:T(8,128)(2,1)}), bf16[32,32,768]{2,1,0:T(8,128)(2,1)S(1)}, u32[]{:S(2)}, u32[]{:S(2)}) async-start(bf16[32,32,768]{2,1,0:T(8,128)(2,1)} %bitcast.41), calls=%async_computation.2 | async-start | bytes 3145728 | tf_op jit(solution)/shard_map/all_to_all | solution.py:66
  118.7 28.4 %copy-start.5 = (f32[64,256]{1,0:T(8,128)S(1)}, f32[64,256]{1,0:T(8,128)}, u32[]{:S(2)}) copy-start(f32[64,256]{1,0:T(8,128)} %get-tuple-element.107) | copy-start | bytes 196612
  146.8 2.1 copy-start.8
  146.8 2.2 copy-start.10
  147.6 5.7 %collective-permute-start.1 = (bf16[64,768]{1,0:T(8,128)(2,1)S(1)}, bf16[64,768]{1,0:T(8,128)(2,1)S(1)}, u32[]{:S(2)}, u32[]{:S(2)}) collective-permute-start(bf16[64,768]{1,0:T(8,128)(2,1)S(1)} %fusion.46), channel_id=1, source_target_pairs={{0,32},{32,64},{64,96},{1,33},{33,65},{65,97},{2,34},{34,66},{66,9... | collective-permute-start | bytes 294920 | tf_op jit(solution)/shard_map/ppermute | solution.py:10
  162.4 28.4 %all-to-all-start.4 = ((bf16[32,32,768]{2,1,0:T(8,128)(2,1)}), bf16[32,32,768]{2,1,0:T(8,128)(2,1)S(1)}, u32[]{:S(2)}, u32[]{:S(2)}) async-start(bf16[32,32,768]{2,1,0:T(8,128)(2,1)} %bitcast.50), calls=%async_computation.4 | async-start | bytes 3145728 | tf_op jit(solution)/shard_map/all_to_all | solution.py:66
  192.4 27.0 %all-to-all-start.5 = ((bf16[32,32,768]{2,1,0:T(8,128)(2,1)}), bf16[32,32,768]{2,1,0:T(8,128)(2,1)S(1)}, u32[]{:S(2)}, u32[]{:S(2)}) async-start(bf16[32,32,768]{2,1,0:T(8,128)(2,1)} %bitcast.53), calls=%async_computation.5 | async-start | bytes 3145728 | tf_op jit(solution)/shard_map/all_to_all | solution.py:91
  198.1 23.4 %copy-start.7 = (f32[64,2]{0,1:T(2,128)S(1)}, f32[64,2]{0,1:T(2,128)}, u32[]{:S(2)}) copy-start(f32[64,2]{0,1:T(2,128)} %get-tuple-element.122) | copy-start | bytes 1540
  220.2 2.0 copy-start.1
  220.2 123.0 %collective-permute-start.2 = (bf16[64,768]{1,0:T(8,128)(2,1)S(1)}, bf16[64,768]{1,0:T(8,128)(2,1)S(1)}, u32[]{:S(2)}, u32[]{:S(2)}) collective-permute-start(bf16[64,768]{1,0:T(8,128)(2,1)S(1)} %fusion.47), channel_id=1, source_target_pairs={{0,32},{32,64},{64,96},{1,33},{33,65},{65,97},{2,34},{34,66},{66,9... | collective-permute-start | bytes 294920 | tf_op jit(solution)/shard_map/ppermute | solution.py:10
  354.4 27.6 %all-to-all-start.6 = ((bf16[32,32,768]{2,1,0:T(8,128)(2,1)}), bf16[32,32,768]{2,1,0:T(8,128)(2,1)S(1)}, u32[]{:S(2)}, u32[]{:S(2)}) async-start(bf16[32,32,768]{2,1,0:T(8,128)(2,1)} %bitcast.59), calls=%async_computation.6 | async-start | bytes 3145728 | tf_op jit(solution)/shard_map/all_to_all | solution.py:66
  423.4 28.4 %copy-start.6 = (f32[64,256]{1,0:T(8,128)S(1)}, f32[64,256]{1,0:T(8,128)}, u32[]{:S(2)}) copy-start(f32[64,256]{1,0:T(8,128)} %get-tuple-element.103) | copy-start | bytes 196612
  451.6 2.1 copy-start.9
  452.4 5.7 %collective-permute-start.3 = (bf16[64,768]{1,0:T(8,128)(2,1)S(1)}, bf16[64,768]{1,0:T(8,128)(2,1)S(1)}, u32[]{:S(2)}, u32[]{:S(2)}) collective-permute-start(bf16[64,768]{1,0:T(8,128)(2,1)S(1)} %fusion.48), channel_id=1, source_target_pairs={{0,32},{32,64},{64,96},{1,33},{33,65},{65,97},{2,34},{34,66},{66,9... | collective-permute-start | bytes 294920 | tf_op jit(solution)/shard_map/ppermute | solution.py:10
  467.1 28.5 %all-to-all-start.8 = ((bf16[32,32,768]{2,1,0:T(8,128)(2,1)}), bf16[32,32,768]{2,1,0:T(8,128)(2,1)S(1)}, u32[]{:S(2)}, u32[]{:S(2)}) async-start(bf16[32,32,768]{2,1,0:T(8,128)(2,1)} %bitcast.68), calls=%async_computation.8 | async-start | bytes 3145728 | tf_op jit(solution)/shard_map/all_to_all | solution.py:66
  538.1 27.0 %all-to-all-start.9 = ((bf16[32,32,768]{2,1,0:T(8,128)(2,1)}), bf16[32,32,768]{2,1,0:T(8,128)(2,1)S(1)}, u32[]{:S(2)}, u32[]{:S(2)}) async-start(bf16[32,32,768]{2,1,0:T(8,128)(2,1)} %bitcast.71), calls=%async_computation.9 | async-start | bytes 3145728 | tf_op jit(solution)/shard_map/all_to_all | solution.py:91
  543.6 22.2 %copy-start.2 = (bf16[64,768]{1,0:T(8,128)(2,1)S(1)}, bf16[64,768]{1,0:T(8,128)(2,1)}, u32[]{:S(2)}) copy-start(bf16[64,768]{1,0:T(8,128)(2,1)} %copy-done.1) | copy-start | bytes 294916
  543.6 22.2 %copy-start.4 = (bf16[64,768]{1,0:T(8,128)(2,1)S(1)}, bf16[64,768]{1,0:T(8,128)(2,1)}, u32[]{:S(2)}) copy-start(bf16[64,768]{1,0:T(8,128)(2,1)} %copy-done.3) | copy-start | bytes 294916
where the time goes:
time: 578 us; the launch traced here: 567 us
  waiting for transfers between devices  299 us (52%)
  blocking collectives  97.8 us (17%)
  local copies, waits for them, and re-layouts  64.1 us (11%)
  starting transfers between devices  55.9 us (10%)
  matrix products  38.9 us (7%)
  other arithmetic  9.36 us (2%)
    ppermute x4, waiting for transfers between devices, passed_along(): lax.ppermute(value, axis, [(source, source + steps) for source in range(i...  133 us
    all_to_all x5, waiting for transfers between devices, on_device(): lax.all_to_all(copies, ('expert', 'tensor'), split_axis=0, concat_axis=0,...  107 us
    all_to_all x3, waiting for transfers between devices, on_device(): lax.all_to_all(partials, ('expert', 'tensor'), split_axis=0, concat_axis=...  59.3 us
    all_to_all x2, blocking collectives, on_device(): lax.all_to_all(partials, ('expert', 'tensor'), split_axis=0, concat_axis=...  56.2 us
    another operation x2, local copies, waits for them, and re-layouts, expert_work(): down_local.reshape(hidden_local, tensor_count, quarter)  46.9 us
    psum x5, blocking collectives, on_device(): squares = lax.psum(jnp.sum(stream_f * stream_f, axis=1), 'tensor')  41.6 us
    all_to_all x5, starting transfers between devices, on_device(): lax.all_to_all(copies, ('expert', 'tensor'), split_axis=0, concat_axis=0,...  34.1 us
    dot_general x2, matrix products, expert_work(): jnp.einsum('ecf,ftd->etcd', hidden.reshape(expert_count, capacity, hidden...  17.2 us
  transfers between devices with their start and end apart: 12, of which 12 were waited for; matrix products, arithmetic and copies ran while one was open for 1% of the time, Pallas kernels for 0%

commit v1 on v0

v1 whole, which is shorter than its diff:
```python
import functools

import jax
import jax.numpy as jnp
from jax import lax
from jax.experimental import pallas as pl
from jax.experimental.pallas import tpu as pltpu
from jax.sharding import PartitionSpec as P

MESH = pl.DeviceIdType.MESH
RING = 4
CAP = 32
F32 = jnp.float32
BF16 = jnp.bfloat16


def relay_kernel(
    inp, meta, gain, up_hbm, down_hbm, out,
    wup, wdn, xbuf, obuf, pbuf, r1, r2, r3, r4, res, xg, hid, dmat, pmat, gslot, mbuf, gbuf, chosen,
    w_sem, m_send, m_recv, n_send, n_recv, z_send, z_recv,
    gf_recv, gg_recv, gp_recv, g_send, sp_recv, s1_recv, s2_recv, s3_recv, s4_recv, s_send,
):
    s = lax.axis_index("segment")
    e = lax.axis_index("expert")
    t = lax.axis_index("tensor")
    segments = lax.axis_size("segment")
    rows, quarter = inp.shape[1], inp.shape[2]
    half = rows // 2
    width = quarter * RING
    hidden = wup.shape[1]
    batches = inp.shape[0]
    y = e // 2
    c = e - 2 * y
    f = t * (1 - c) + y * c
    g = y * (1 - c) + t * c

    def mod4(v):
        return lax.rem(v + 8, 4)

    def device(df, dg):
        nf, ng = mod4(f + df), mod4(g + dg)
        nt = nf * (1 - c) + ng * c
        ny = ng * (1 - c) + nf * c
        return {"tensor": nt, "expert": 2 * ny + c}

    partner = {"expert": 2 * y + (1 - c)}
    above = {"segment": lax.rem(s + 1, segments)}
    below = {"segment": lax.rem(s + segments - 1, segments)}

    def place(gi, fi):
        q = fi * (1 - c) + gi * c
        yy = gi * (1 - c) + fi * c
        return q * RING + yy

    def send(src, dst, send_sem, recv_sem, where):
        pltpu.make_async_remote_copy(
            src_ref=src, dst_ref=dst, send_sem=send_sem, recv_sem=recv_sem, device_id=where, device_id_type=MESH
        ).start()

    def arrive(ref, sem):
        pltpu.make_async_copy(ref, ref, sem).wait()

    up_copy = pltpu.make_async_copy(up_hbm, wup, w_sem.at[0])
    down_copy = pltpu.make_async_copy(down_hbm, wdn, w_sem.at[1])
    up_copy.start()
    down_copy.start()

    barrier = pltpu.get_barrier_semaphore()
    for step in range(1, 8):
        pl.semaphore_signal(barrier, inc=1, device_id={"expert": lax.rem(e + step, 8)}, device_id_type=MESH)
    for step in range(1, RING):
        pl.semaphore_signal(barrier, inc=1, device_id={"tensor": lax.rem(t + step, RING)}, device_id_type=MESH)
    pl.semaphore_signal(barrier, inc=1, device_id=above, device_id_type=MESH)
    pl.semaphore_signal(barrier, inc=1, device_id=below, device_id_type=MESH)
    pl.semaphore_wait(barrier, 12)

    @pl.when(s == 0)
    def _():
        for m in range(batches):
            pltpu.make_async_copy(inp.at[m], xbuf.at[(m * 2 + c) * 16 + place(g, f)], z_recv.at[m]).start()

    for step in range(1, 8):
        send(meta, mbuf.at[e], m_send.at[step - 1], m_recv.at[step - 1], {"expert": lax.rem(e + step, 8)})
    for step in range(1, RING):
        send(gain, gbuf.at[t], n_send.at[step - 1], n_recv.at[step - 1], {"tensor": lax.rem(t + step, RING)})
    own_meta = pltpu.make_async_copy(meta, mbuf.at[e], m_send.at[7])
    own_gain = pltpu.make_async_copy(gain, gbuf.at[t], n_send.at[3])
    own_meta.start()
    own_gain.start()

    def gather_first(m):
        base = (m * 2 + c) * 16
        full = lambda fi: xbuf.at[base + place(g, fi)]
        lower = lambda fi: xbuf.at[base + place(g, fi), pl.ds(0, half)]
        upper = lambda fi: xbuf.at[base + place(g, fi), pl.ds(half, half)]
        f_up, f_dn, f_far = mod4(f + 1), mod4(f - 1), mod4(f + 2)
        order = (f, f_dn, f_up, f_far)
        arrive(full(f), z_recv.at[m])
        send(full(f), full(f), g_send.at[m], gf_recv.at[m, 0], device(1, 0))
        send(full(f), full(f), g_send.at[m], gf_recv.at[m, 1], device(-1, 0))

        def spread(fi, number):
            ref = full(fi)
            send(ref, ref, g_send.at[m], gg_recv.at[m, number, 0], device(0, 1))
            send(ref, ref, g_send.at[m], gg_recv.at[m, number, 1], device(0, -1))
            send(ref, ref, g_send.at[m], gp_recv.at[m], partner)

        spread(f, 0)
        arrive(full(f_dn), gf_recv.at[m, 0])
        send(lower(f_dn), lower(f_dn), g_send.at[m], gf_recv.at[m, 2], device(1, 0))
        spread(f_dn, 1)
        arrive(full(f_up), gf_recv.at[m, 1])
        send(upper(f_up), upper(f_up), g_send.at[m], gf_recv.at[m, 3], device(-1, 0))
        spread(f_up, 2)
        arrive(lower(f_far), gf_recv.at[m, 2])
        arrive(upper(f_far), gf_recv.at[m, 3])
        spread(f_far, 3)

        for number, fi in enumerate(order):
            from_dn = lambda gi: xbuf.at[base + place(gi, fi)]
            ref = from_dn(mod4(g - 1))
            arrive(ref, gg_recv.at[m, number, 0])
            part = xbuf.at[base + place(mod4(g - 1), fi), pl.ds(0, half)]
            send(part, part, g_send.at[m], gg_recv.at[m, number, 2], device(0, 1))
            send(ref, ref, g_send.at[m], gp_recv.at[m], partner)
            ref = from_dn(mod4(g + 1))
            arrive(ref, gg_recv.at[m, number, 1])
            part = xbuf.at[base + place(mod4(g + 1), fi), pl.ds(half, half)]
            send(part, part, g_send.at[m], gg_recv.at[m, number, 3], device(0, -1))
            send(ref, ref, g_send.at[m], gp_recv.at[m], partner)
        for number, fi in enumerate(order):
            spot = base + place(mod4(g + 2), fi)
            arrive(xbuf.at[spot, pl.ds(0, half)], gg_recv.at[m, number, 2])
            arrive(xbuf.at[spot, pl.ds(half, half)], gg_recv.at[m, number, 3])
            send(xbuf.at[spot], xbuf.at[spot], g_send.at[m], gp_recv.at[m], partner)
        arrive(xbuf.at[pl.ds((m * 2 + 1 - c) * 16, 16)], gp_recv.at[m])

    def set_up_routing(m):
        slots = RING * CAP
        tokens = RING * rows
        mine = e.astype(F32)
        row_i = lax.broadcasted_iota(jnp.int32, (tokens, tokens), 0)
        col_i = lax.broadcasted_iota(jnp.int32, (tokens, tokens), 1)
        earlier = ((row_i < col_i) & (row_i // rows == col_i // rows)).astype(BF16)
        slot_id = lax.broadcasted_iota(jnp.int32, (slots, tokens), 0).astype(F32)
        first_slot = (lax.broadcasted_iota(jnp.int32, (1, tokens), 1) // rows * CAP).astype(F32)
        for p in range(2):
            table = jnp.concatenate([mbuf[p] + mbuf[2 + p], mbuf[4 + p] + mbuf[6 + p]], axis=1)
            for mb in range(batches):
                hit0 = table[2 * mb:2 * mb + 1] == mine
                hit1 = table[2 * mb + 1:2 * mb + 2] == mine
                named = jnp.where(hit0 | hit1, 1.0, 0.0)
                chosen[...] = jnp.broadcast_to(named, chosen.shape).astype(BF16)
                before = jnp.dot(chosen[...], earlier, preferred_element_type=F32)[0:1]
                position = jnp.where(named > 0.0, before + first_slot, -1.0)
                gate = jnp.where(hit0, table[4 + 2 * mb:5 + 2 * mb], 0.0) + jnp.where(
                    hit1, table[5 + 2 * mb:6 + 2 * mb], 0.0
                )
                onehot = jnp.where(slot_id == position, 1.0, 0.0)
                dmat[mb, p] = onehot.astype(BF16)
                pmat[mb, p] = onehot.T.astype(BF16)
                gslot[mb, pl.ds(p * slots, slots)] = jnp.sum(onehot * gate, axis=1, keepdims=True)

    def experts(m):
        slots = RING * CAP
        total = [jnp.zeros((slots, 1), F32) for _ in range(2)]
        for q in range(RING):
            for p in range(2):
                tokens = xbuf[pl.ds((m * 2 + p) * 16 + q * RING, RING)].reshape(RING * rows, quarter)
                picked = jnp.dot(dmat[m, p], tokens, preferred_element_type=F32)
                total[p] += jnp.sum(picked * picked, axis=1, keepdims=True)
                xg[p * slots:(p + 1) * slots, q * quarter:(q + 1) * quarter] = (picked * gbuf[q, 0:1]).astype(BF16)
        scale = lax.rsqrt(jnp.concatenate(total, axis=0) / width + 1e-05)
        weight = gslot[m]
        step = hidden // 4

        def up(i, carry):
            cols = pl.ds(pl.multiple_of(i * step, step), step)
            v = jnp.dot(xg[...], wup[:, cols], preferred_element_type=F32) * scale
            hid[:, cols] = (v / (1.0 + jnp.exp(-v)) * weight).astype(BF16)
            return carry

        lax.fori_loop(0, 4, up, 0)

    def chunk(number):
        return mod4(t + (2, -1, 1, 0)[number])

    def down(m, number):
        slots = RING * CAP
        q = chunk(number)
        cols = pl.ds(pl.multiple_of(q * quarter, quarter), quarter)
        part = jnp.dot(hid[...], wdn[:, cols], preferred_element_type=F32).astype(BF16)
        for p in range(2):
            value = jnp.dot(pmat[m, p], part[p * slots:(p + 1) * slots], preferred_element_type=F32)
            obuf[pl.ds(p * 16 + q * RING, RING)] = value.astype(BF16).reshape(RING, rows, quarter)
        send(
            obuf.at[pl.ds((1 - c) * 16 + q * RING, RING)], pbuf.at[m, pl.ds(q * RING, RING)],
            s_send.at[m], sp_recv.at[m, number], partner,
        )

    def join(m, number):
        q = chunk(number)
        arrive(pbuf.at[m, pl.ds(q * RING, RING)], sp_recv.at[m, number])
        mine = pl.ds(c * 16 + q * RING, RING)
        obuf[mine] = (obuf[mine].astype(F32) + pbuf[m, pl.ds(q * RING, RING)].astype(F32)).astype(BF16)

    def scatter(m):
        own = c * 16
        f_far, f_dn, f_up = mod4(f + 2), mod4(f - 1), mod4(f + 1)
        order = (f_far, f_dn, f_up, f)
        low, high = pl.ds(0, half), pl.ds(half, half)
        for number, fi in enumerate(order):
            spot = own + place(mod4(g + 2), fi)
            send(obuf.at[spot, low], r1.at[m, 0, number], s_send.at[m], s1_recv.at[m, number, 0], device(0, 1))
            send(obuf.at[spot, high], r1.at[m, 1, number], s_send.at[m], s1_recv.at[m, number, 1], device(0, -1))
        for number, fi in enumerate(order):
            for side, dg, part in ((0, 1, low), (1, -1, high)):
                spot = own + place(mod4(g + dg), fi)
                arrive(r1.at[m, side, number], s1_recv.at[m, number, side])
                obuf[spot, part] = (obuf[spot, part].astype(F32) + r1[m, side, number].astype(F32)).astype(BF16)
                send(obuf.at[spot], r2.at[m, side, number], s_send.at[m], s2_recv.at[m, number, side], device(0, dg))
        for number, fi in enumerate(order):
            spot = own + place(g, fi)
            arrive(r2.at[m, 0, number], s2_recv.at[m, number, 0])
            arrive(r2.at[m, 1, number], s2_recv.at[m, number, 1])
            if number in (1, 2):
                side, df, part = ((1, -1, high), (0, 1, low))[number - 1]
            total = obuf[spot].astype(F32) + r2[m, 0, number].astype(F32) + r2[m, 1, number].astype(F32)
            if number == 0:
                obuf[spot] = total.astype(BF16)
                send(obuf.at[spot, low], r3.at[m, 0], s_send.at[m], s3_recv.at[m, 0], device(1, 0))
                send(obuf.at[spot, high], r3.at[m, 1], s_send.at[m], s3_recv.at[m, 1], device(-1, 0))
            elif number == 3:
                final = total
            else:
                obuf[spot] = total.astype(BF16)
                arrive(r3.at[m, side], s3_recv.at[m, side])
                obuf[spot, part] = (obuf[spot, part].astype(F32) + r3[m, side].astype(F32)).astype(BF16)
                send(obuf.at[spot], r4.at[m, side], s_send.at[m], s4_recv.at[m, side], device(df, 0))
        arrive(r4.at[m, 0], s4_recv.at[m, 0])
        arrive(r4.at[m, 1], s4_recv.at[m, 1])
        stream = xbuf[(m * 2 + c) * 16 + place(g, f)].astype(F32)
        result = (stream + (final + r4[m, 0].astype(F32) + r4[m, 1].astype(F32))).astype(BF16)
        res[m] = result
        out[m] = result

        @pl.when(s < segments - 1)
        def _():
            send(res.at[m], xbuf.at[(m * 2 + c) * 16 + place(g, f)], z_send.at[m], z_recv.at[m], above)

    def one_batch(m, carry):
        gather_first(m)

        @pl.when(m == 0)
        def _():
            for step in range(7):
                arrive(meta, m_recv.at[step])
            for step in range(3):
                arrive(gain, n_recv.at[step])
            own_meta.wait()
            own_gain.wait()
            set_up_routing(m)
            up_copy.wait()
            down_copy.wait()

        experts(m)
        for number in range(RING):
            down(m, number)
        for number in range(RING):
            join(m, number)
        scatter(m)
        arrive(xbuf.at[pl.ds(0, 31)], g_send.at[m])
        arrive(xbuf.at[pl.ds(0, 31)], s_send.at[m])
        return carry

    lax.fori_loop(0, batches, one_batch, 0)

    for step in range(7):
        arrive(meta, m_send.at[step])
    for step in range(3):
        arrive(gain, n_send.at[step])

    @pl.when(s < segments - 1)
    def _():
        for m in range(batches):
            arrive(res.at[m], z_send.at[m])


def on_device(inputs, norm_gain, up_weight, down_weight, routing, gates):
    batches, rows, quarter = inputs.shape
    width, hidden = up_weight.shape[2:]
    lanes = 2 * rows
    choice_rows = routing[0].astype(F32).transpose(0, 2, 1).reshape(2 * batches, rows)
    gate_rows = gates[0].transpose(0, 2, 1).reshape(2 * batches, rows)
    both = jnp.concatenate([choice_rows, gate_rows], axis=0)
    place = lax.rem(lax.axis_index("expert") // 2, 2)
    filled = jnp.concatenate([both, both], axis=1)
    meta = jnp.where(jnp.arange(lanes)[None, :] // rows == place, filled, 0.0)
    gain = jnp.broadcast_to(norm_gain, (8, quarter))
    slots = RING * CAP
    half = rows // 2
    dma = pltpu.SemaphoreType.DMA
    vmem = pl.BlockSpec(memory_space=pltpu.VMEM)
    hbm = pl.BlockSpec(memory_space=pl.ANY)
    result = pl.pallas_call(
        relay_kernel,
        out_shape=jax.ShapeDtypeStruct((batches, rows, quarter), BF16),
        in_specs=[vmem, vmem, vmem, hbm, hbm],
        out_specs=vmem,
        scratch_shapes=[
            pltpu.VMEM((width, hidden), BF16),
            pltpu.VMEM((hidden, width), BF16),
            pltpu.VMEM((batches * 2 * 16, rows, quarter), BF16),
            pltpu.VMEM((2 * 16, rows, quarter), BF16),
            pltpu.VMEM((batches, 16, rows, quarter), BF16),
            pltpu.VMEM((batches, 2, RING, half, quarter), BF16),
            pltpu.VMEM((batches, 2, RING, rows, quarter), BF16),
            pltpu.VMEM((batches, 2, half, quarter), BF16),
            pltpu.VMEM((batches, 2, rows, quarter), BF16),
            pltpu.VMEM((batches, rows, quarter), BF16),
            pltpu.VMEM((2 * slots, width), BF16),
            pltpu.VMEM((2 * slots, hidden), BF16),
            pltpu.VMEM((batches, 2, slots, RING * rows), BF16),
            pltpu.VMEM((batches, 2, RING * rows, slots), BF16),
            pltpu.VMEM((batches, 2 * slots, 1), F32),
            pltpu.VMEM((8, 8, lanes), F32),
            pltpu.VMEM((RING, 8, quarter), F32),
            pltpu.VMEM((16, RING * rows), BF16),
            dma((2,)),
            dma((8,)),
            dma((7,)),
            dma((4,)),
            dma((3,)),
            dma((batches,)),
            dma((batches,)),
            dma((batches, 4)),
            dma((batches, RING, 4)),
            dma((batches,)),
            dma((batches,)),
            dma((batches, RING)),
            dma((batches, RING, 2)),
            dma((batches, RING, 2)),
            dma((batches, 2)),
            dma((batches, 2)),
            dma((batches,)),
        ],
        compiler_params=pltpu.CompilerParams(
            collective_id=0, has_side_effects=True, vmem_limit_bytes=67043328
        ),
    )(inputs, meta, gain, up_weight.reshape(width, hidden), down_weight.reshape(hidden, width))
    return result[None]


def solution(mesh):
    return jax.shard_map(
        on_device,
        mesh=mesh,
        in_specs=(
            P(None, "expert", "tensor"),
            P("segment", "tensor"),
            P("segment", "expert", None, "tensor"),
            P("segment", "expert", "tensor", None),
            P("segment", None, "expert", None),
            P("segment", None, "expert", None),
        ),
        out_specs=P("segment", None, "expert", "tensor"),
        check_vma=False,
    )
```

time: 578 us -> 256 us (0.44); the launches traced: 567 us -> 252 us
  waiting for transfers between devices: 299 us -> 0 us
  Pallas kernels: 0 us -> 247 us
  blocking collectives: 97.8 us -> 0 us
  local copies, waits for them, and re-layouts: 64.1 us -> 2.23 us
  starting transfers between devices: 55.9 us -> 0 us
  matrix products: 38.9 us -> 0 us
  other arithmetic: 9.36 us -> 2.8 us
    pallas_call x0 -> x1, Pallas kernels: none -> 247 us  [on_device(): pl.pallas_call(relay_kernel, out_shape=jax.ShapeDtypeStruct((batches, row...]
    all_to_all x8 -> x0, waiting for transfers between devices: 166 us -> none  [the longest x5 107 us: on_device(): lax.all_to_all(copies, ('expert', 'tensor'), split_axis=0, concat_axis=0,...]
    ppermute x4 -> x0, waiting for transfers between devices: 133 us -> none  [passed_along(): lax.ppermute(value, axis, [(source, source + steps) for source in range(i...]
    all_to_all x2 -> x0, blocking collectives: 56.2 us -> none  [on_device(): lax.all_to_all(partials, ('expert', 'tensor'), split_axis=0, concat_axis=...]
    another operation x7 -> x0, local copies, waits for them, and re-layouts: 52.3 us -> none  [the longest x2 46.9 us: expert_work(): down_local.reshape(hidden_local, tensor_count, quarter)]
    all_to_all x8 -> x0, starting transfers between devices: 50.7 us -> none  [the longest x5 34.1 us: on_device(): lax.all_to_all(copies, ('expert', 'tensor'), split_axis=0, concat_axis=0,...]
    psum x5 -> x0, blocking collectives: 41.6 us -> none  [on_device(): squares = lax.psum(jnp.sum(stream_f * stream_f, axis=1), 'tensor')]
    dot_general x14 -> x0, matrix products: 38.9 us -> none  [the longest x2 17.2 us: expert_work(): jnp.einsum('ecf,ftd->etcd', hidden.reshape(expert_count, capacity, hidden...]
  transfers between devices with their start and end apart: 12 -> 0, of which waited for: 12 -> 0; matrix products, arithmetic and copies ran while one was open for 1% -> 0% of each run, Pallas kernels for 0% -> 0%
where the time goes in v1:
time: 256 us; the launch traced here: 252 us
  Pallas kernels  247 us (96%)
  other arithmetic  2.8 us (1%)
    pallas_call x1, Pallas kernels, on_device(): pl.pallas_call(relay_kernel, out_shape=jax.ShapeDtypeStruct((batches, row...  247 us

profile of v1, /device:TPU:97, one launch (start us, length us, event | category | flops | bytes accessed | tf_op | source)
XLA Modules:
  0.0 252.4 jit_solution(12919265123000243896)
XLA Ops:
  0.0 0.7 convert_element_type.6
  0.7 1.4 maximum_select_fusion.meta
  2.1 0.7 reduce
  2.8 0.6 broadcast_in_dim.26.gain
  3.4 247.4 %shard_map.64 = bf16[2,64,768]{2,1,0:T(8,128)(2,1)} custom-call(bf16[2,64,768]{2,1,0:T(8,128)(2,1)} %inp.1, f32[8,128]{1,0:T(8,128)} %maximum_select_fusion.meta, f32[8,768]{1,0:T(8,128)} %broadcast_in_dim.26.gain, bf16[3072,2048]{1,0:T(8,128)(2,1)} %bitcast.13, bf16[2048,3072]{1,0:T(8,128)(2,1)} %bitcast.14), custom_call_target="tpu_custom_call" | custom-call | tf_op jit(solution)/shard_map/pallas_call | solution.py:305
  250.8 1.6 copy.8
  (1 shorter events, 0.0 us)

commit v2 on v1

v2 whole, which is shorter than its diff:
```python
import functools

import jax
import jax.numpy as jnp
from jax import lax
from jax.experimental import pallas as pl
from jax.experimental.pallas import tpu as pltpu
from jax.sharding import PartitionSpec as P

MESH = pl.DeviceIdType.MESH
RING = 4
CAP = 32
F32 = jnp.float32
BF16 = jnp.bfloat16


def relay_kernel(
    inp, meta, gain, up_hbm, down_hbm, out,
    wup, wdn, xbuf, obuf, pbuf, r2, r3, res, xg, acc, squares, hid, dmat, pmat, gslot, mbuf, gbuf, chosen,
    w_sem, m_send, m_recv, n_send, n_recv, z_send, z_recv,
    gf_recv, gg_recv, gp_recv, f_send, g_send, sp_recv, s2_recv, s3_recv, s_send,
):
    s = lax.axis_index("segment")
    e = lax.axis_index("expert")
    t = lax.axis_index("tensor")
    segments = lax.axis_size("segment")
    rows, quarter = inp.shape[1], inp.shape[2]
    width = quarter * RING
    hidden = wup.shape[1]
    batches = inp.shape[0]
    y = e // 2
    c = e - 2 * y
    f = t * (1 - c) + y * c
    g = y * (1 - c) + t * c

    def part(h):
        return pl.ds(h * (rows // 2), rows // 2)

    def mod4(v):
        return lax.rem(v + 8, 4)

    def device(df, dg):
        nf, ng = mod4(f + df), mod4(g + dg)
        nt = nf * (1 - c) + ng * c
        ny = ng * (1 - c) + nf * c
        return {"tensor": nt, "expert": 2 * ny + c}

    partner = {"expert": 2 * y + (1 - c)}
    above = {"segment": lax.rem(s + 1, segments)}
    below = {"segment": lax.rem(s + segments - 1, segments)}

    def place(gi, fi):
        q = fi * (1 - c) + gi * c
        yy = gi * (1 - c) + fi * c
        return q * RING + yy

    def send(src, dst, send_sem, recv_sem, where):
        pltpu.make_async_remote_copy(
            src_ref=src, dst_ref=dst, send_sem=send_sem, recv_sem=recv_sem, device_id=where, device_id_type=MESH
        ).start()

    def arrive(ref, sem):
        pltpu.make_async_copy(ref, ref, sem).wait()

    up_copy = pltpu.make_async_copy(up_hbm, wup, w_sem.at[0])
    down_copy = pltpu.make_async_copy(down_hbm, wdn, w_sem.at[1])
    up_copy.start()

    barrier = pltpu.get_barrier_semaphore()
    for step in range(1, 8):
        pl.semaphore_signal(barrier, inc=1, device_id={"expert": lax.rem(e + step, 8)}, device_id_type=MESH)
    for step in range(1, RING):
        pl.semaphore_signal(barrier, inc=1, device_id={"tensor": lax.rem(t + step, RING)}, device_id_type=MESH)
    pl.semaphore_signal(barrier, inc=1, device_id=above, device_id_type=MESH)
    pl.semaphore_signal(barrier, inc=1, device_id=below, device_id_type=MESH)
    pl.semaphore_wait(barrier, 12)
    down_copy.start()

    @pl.when(s == 0)
    def _():
        for m in range(batches):
            for h in range(2):
                here = xbuf.at[(m * 2 + c) * 16 + place(g, f), part(h)]
                pltpu.make_async_copy(inp.at[m, part(h)], here, z_recv.at[m, h]).start()

    for step in range(1, 8):
        send(meta, mbuf.at[e], m_send.at[step - 1], m_recv.at[step - 1], {"expert": lax.rem(e + step, 8)})
    for step in range(1, RING):
        send(gain, gbuf.at[t], n_send.at[step - 1], n_recv.at[step - 1], {"tensor": lax.rem(t + step, RING)})
    own_meta = pltpu.make_async_copy(meta, mbuf.at[e], m_send.at[7])
    own_gain = pltpu.make_async_copy(gain, gbuf.at[t], n_send.at[3])
    own_meta.start()
    own_gain.start()

    slots = RING * CAP
    tokens = RING * rows
    f_far, f_dn, f_up = mod4(f + 2), mod4(f - 1), mod4(f + 1)
    g_far, g_dn, g_up = mod4(g + 2), mod4(g - 1), mod4(g + 1)

    def gather_steps(m):
        base = (m * 2 + c) * 16
        order = (f, f_dn, f_up, f_far)

        def to_partner(ref, number, g_number):
            group = number * (1 - c) + g_number * c
            send(ref, ref, g_send.at[m], gp_recv.at[m, group], partner)

        def spread(number):
            ref = xbuf.at[base + place(g, order[number])]
            for kind, dg in enumerate((1, -1, 2)):
                send(ref, ref, g_send.at[m], gg_recv.at[m, number, kind], device(0, dg))
            to_partner(ref, number, 0)

        def pass_on(number, kinds=(0, 1, 2)):
            for kind in kinds:
                ref = xbuf.at[base + place((g_dn, g_up, g_far)[kind], order[number])]
                arrive(ref, gg_recv.at[m, number, kind])
                to_partner(ref, number, 1 + kind)

        def start():
            for h in range(2):
                own = xbuf.at[base + place(g, f), part(h)]
                arrive(own, z_recv.at[m, h])
                for kind, df in ((2, 2), (0, 1), (1, -1)):
                    send(own, own, f_send.at[m], gf_recv.at[m, kind, h], device(df, 0))
            arrive(xbuf.at[pl.ds(0, 3)], f_send.at[m])
            spread(0)

        def turn():
            for number, fi in ((1, f_dn), (2, f_up), (3, f_far)):
                for h in range(2):
                    arrive(xbuf.at[base + place(g, fi), part(h)], gf_recv.at[m, number - 1, h])
                spread(number)

        return start, turn, pass_on

    def set_up_routing():
        for step in range(7):
            arrive(meta, m_recv.at[step])
        for step in range(3):
            arrive(gain, n_recv.at[step])
        own_meta.wait()
        own_gain.wait()
        mine = e.astype(F32)
        row_i = lax.broadcasted_iota(jnp.int32, (tokens, tokens), 0)
        col_i = lax.broadcasted_iota(jnp.int32, (tokens, tokens), 1)
        earlier = ((row_i < col_i) & (row_i // rows == col_i // rows)).astype(BF16)
        slot_id = lax.broadcasted_iota(jnp.int32, (slots, tokens), 0).astype(F32)
        first_slot = (lax.broadcasted_iota(jnp.int32, (1, tokens), 1) // rows * CAP).astype(F32)
        for p in range(2):
            table = jnp.concatenate([mbuf[p] + mbuf[2 + p], mbuf[4 + p] + mbuf[6 + p]], axis=1)
            for mb in range(batches):
                hit0 = table[2 * mb:2 * mb + 1] == mine
                hit1 = table[2 * mb + 1:2 * mb + 2] == mine
                named = jnp.where(hit0 | hit1, 1.0, 0.0)
                chosen[...] = jnp.broadcast_to(named, chosen.shape).astype(BF16)
                before = jnp.dot(chosen[...], earlier, preferred_element_type=F32)[0:1]
                position = jnp.where(named > 0.0, before + first_slot, -1.0)
                gate = jnp.where(hit0, table[4 + 2 * mb:5 + 2 * mb], 0.0) + jnp.where(
                    hit1, table[5 + 2 * mb:6 + 2 * mb], 0.0
                )
                onehot = jnp.where(slot_id == position, 1.0, 0.0)
                dmat[mb, p] = onehot.astype(BF16)
                pmat[mb, p] = onehot.T.astype(BF16)
                gslot[mb, pl.ds(p * slots, slots)] = jnp.sum(onehot * gate, axis=1, keepdims=True)

    def up(m, number):
        q = mod4(t + (0, -1, 1, 2)[number])
        theirs = xbuf.at[pl.ds((m * 2 + 1 - c) * 16 + q * RING, RING)]
        arrive(theirs, gp_recv.at[m, number])
        for p in range(2):
            block = xbuf[pl.ds((m * 2 + p) * 16 + q * RING, RING)].reshape(tokens, quarter)
            picked = jnp.dot(dmat[m, p], block, preferred_element_type=F32)
            square = jnp.sum(picked * picked, axis=1, keepdims=True)
            mine = pl.ds(p * slots, slots)
            squares[mine] = square if number == 0 else squares[mine] + square
            xg[mine] = (picked * gbuf[q, 0:1]).astype(BF16)
        step = hidden // 2
        deep = pl.ds(pl.multiple_of(q * quarter, quarter), quarter)
        for i in range(2):
            cols = pl.ds(i * step, step)
            v = jnp.dot(xg[...], wup[deep, cols], preferred_element_type=F32)
            if number > 0:
                v = v + acc[:, cols]
            if number < RING - 1:
                acc[:, cols] = v
            else:
                v = v * lax.rsqrt(squares[...] / width + 1e-05)
                hid[:, cols] = (v / (1.0 + jnp.exp(-v)) * gslot[m]).astype(BF16)

    def chunk(number):
        return mod4(t + (2, -1, 1, 0)[number])

    def down(m, number):
        q = chunk(number)
        cols = pl.ds(pl.multiple_of(q * quarter, quarter), quarter)
        part = jnp.dot(hid[...], wdn[:, cols], preferred_element_type=F32).astype(BF16)
        for p in range(2):
            value = jnp.dot(pmat[m, p], part[p * slots:(p + 1) * slots], preferred_element_type=F32)
            obuf[pl.ds(p * 16 + q * RING, RING)] = value.astype(BF16).reshape(RING, rows, quarter)
        send(
            obuf.at[pl.ds((1 - c) * 16 + q * RING, RING)], pbuf.at[m, pl.ds(q * RING, RING)],
            s_send.at[m], sp_recv.at[m, number], partner,
        )

    def join(m, number):
        q = chunk(number)
        theirs = pl.ds(q * RING, RING)
        arrive(pbuf.at[m, theirs], sp_recv.at[m, number])
        mine = pl.ds(c * 16 + q * RING, RING)
        obuf[mine] = (obuf[mine].astype(F32) + pbuf[m, theirs].astype(F32)).astype(BF16)

    s_order = (f_far, f_dn, f_up, f)

    def to_ring(m, number):
        @pl.when(c == 0)
        def _():
            for kind, dg in ((2, 2), (0, 1), (1, -1)):
                spot = place(mod4(g + dg), s_order[number])
                send(obuf.at[spot], r2.at[m, kind, number], s_send.at[m], s2_recv.at[m, number, kind], device(0, dg))

        if number < RING - 1:
            @pl.when(c == 1)
            def _():
                kind, dg = ((2, 2), (1, -1), (0, 1))[number]
                for n in range(RING):
                    spot = 16 + place(mod4(g + dg), s_order[n])
                    send(obuf.at[spot], r2.at[m, kind, n], s_send.at[m], s2_recv.at[m, n, kind], device(0, dg))

    def second_ring(m, number):
        spot = c * 16 + place(g, s_order[number])
        total = obuf[spot].astype(F32)
        for kind in range(3):
            arrive(r2.at[m, kind, number], s2_recv.at[m, number, kind])
            total += r2[m, kind, number].astype(F32)
        if number == RING - 1:
            return total
        obuf[spot] = total.astype(BF16)
        send(
            obuf.at[spot], r3.at[m, number], s_send.at[m], s3_recv.at[m, number], device((2, -1, 1)[number], 0)
        )

    def finish(m):
        total = second_ring(m, RING - 1)
        for number in range(RING - 1):
            arrive(r3.at[m, number], s3_recv.at[m, number])
        spot = (m * 2 + c) * 16 + place(g, f)
        for h in range(2):
            value = xbuf[spot, part(h)].astype(F32) + total[h * (rows // 2):(h + 1) * (rows // 2)]
            for number in range(RING - 1):
                value += r3[m, number, part(h)].astype(F32)
            res[m, part(h)] = value.astype(BF16)

            @pl.when(s < segments - 1)
            def _():
                send(res.at[m, part(h)], xbuf.at[spot, part(h)], z_send.at[m], z_recv.at[m, h], above)

        out[m] = res[m]

    def project(m):
        down(m, 0)
        down(m, 1)
        join(m, 0)
        to_ring(m, 0)
        down(m, 2)
        join(m, 1)
        to_ring(m, 1)
        down(m, 3)
        join(m, 2)
        to_ring(m, 2)
        join(m, 3)
        to_ring(m, 3)

    def sent(m):
        arrive(xbuf.at[pl.ds(0, 28)], g_send.at[m])
        arrive(xbuf.at[pl.ds(0, 31)], s_send.at[m])

    @pl.when(s > 0)
    def _():
        set_up_routing()
        up_copy.wait()

    def one_batch(m, carry):
        start, turn, pass_on = gather_steps(m)
        start()
        turn()
        pass_on(0)

        @pl.when((s == 0) & (m == 0))
        def _():
            set_up_routing()
            up_copy.wait()

        up(m, 0)
        pass_on(1)
        pass_on(2)
        pass_on(3, (0, 1))
        up(m, 1)
        pass_on(3, (2,))
        up(m, 2)
        up(m, 3)

        @pl.when(m == 0)
        def _():
            down_copy.wait()

        project(m)
        for number in range(RING - 1):
            second_ring(m, number)
        finish(m)
        sent(m)
        return carry

    lax.fori_loop(0, batches, one_batch, 0)

    for step in range(7):
        arrive(meta, m_send.at[step])
    for step in range(3):
        arrive(gain, n_send.at[step])

    @pl.when(s < segments - 1)
    def _():
        for m in range(batches):
            arrive(res.at[m], z_send.at[m])


def on_device(inputs, norm_gain, up_weight, down_weight, routing, gates):
    batches, rows, quarter = inputs.shape
    width, hidden = up_weight.shape[2:]
    lanes = 2 * rows
    choice_rows = routing[0].astype(F32).transpose(0, 2, 1).reshape(2 * batches, rows)
    gate_rows = gates[0].transpose(0, 2, 1).reshape(2 * batches, rows)
    both = jnp.concatenate([choice_rows, gate_rows], axis=0)
    place = lax.rem(lax.axis_index("expert") // 2, 2)
    filled = jnp.concatenate([both, both], axis=1)
    meta = jnp.where(jnp.arange(lanes)[None, :] // rows == place, filled, 0.0)
    gain = jnp.broadcast_to(norm_gain, (8, quarter))
    slots = RING * CAP
    dma = pltpu.SemaphoreType.DMA
    vmem = pl.BlockSpec(memory_space=pltpu.VMEM)
    hbm = pl.BlockSpec(memory_space=pl.ANY)
    result = pl.pallas_call(
        relay_kernel,
        out_shape=jax.ShapeDtypeStruct((batches, rows, quarter), BF16),
        in_specs=[vmem, vmem, vmem, hbm, hbm],
        out_specs=vmem,
        scratch_shapes=[
            pltpu.VMEM((width, hidden), BF16),
            pltpu.VMEM((hidden, width), BF16),
            pltpu.VMEM((batches * 2 * 16, rows, quarter), BF16),
            pltpu.VMEM((2 * 16, rows, quarter), BF16),
            pltpu.VMEM((batches, 16, rows, quarter), BF16),
            pltpu.VMEM((batches, 3, RING, rows, quarter), BF16),
            pltpu.VMEM((batches, RING - 1, rows, quarter), BF16),
            pltpu.VMEM((batches, rows, quarter), BF16),
            pltpu.VMEM((2 * slots, quarter), BF16),
            pltpu.VMEM((2 * slots, hidden), F32),
            pltpu.VMEM((2 * slots, 1), F32),
            pltpu.VMEM((2 * slots, hidden), BF16),
            pltpu.VMEM((batches, 2, slots, RING * rows), BF16),
            pltpu.VMEM((batches, 2, RING * rows, slots), BF16),
            pltpu.VMEM((batches, 2 * slots, 1), F32),
            pltpu.VMEM((8, 8, lanes), F32),
            pltpu.VMEM((RING, 8, quarter), F32),
            pltpu.VMEM((16, RING * rows), BF16),
            dma((2,)),
            dma((8,)),
            dma((7,)),
            dma((4,)),
            dma((3,)),
            dma((batches,)),
            dma((batches, 2)),
            dma((batches, 3, 2)),
            dma((batches, RING, 3)),
            dma((batches, RING)),
            dma((batches,)),
            dma((batches,)),
            dma((batches, RING)),
            dma((batches, RING, 3)),
            dma((batches, RING - 1)),
            dma((batches,)),
        ],
        compiler_params=pltpu.CompilerParams(
            collective_id=0, has_side_effects=True, vmem_limit_bytes=67043328
        ),
    )(inputs, meta, gain, up_weight.reshape(width, hidden), down_weight.reshape(hidden, width))
    return result[None]


def solution(mesh):
    return jax.shard_map(
        on_device,
        mesh=mesh,
        in_specs=(
            P(None, "expert", "tensor"),
            P("segment", "tensor"),
            P("segment", "expert", None, "tensor"),
            P("segment", "expert", "tensor", None),
            P("segment", None, "expert", None),
            P("segment", None, "expert", None),
        ),
        out_specs=P("segment", None, "expert", "tensor"),
        check_vma=False,
    )
```

time: 256 us -> 205 us (0.80); the launches traced: 252 us -> 204 us
  Pallas kernels: 247 us -> 199 us
    pallas_call x1, Pallas kernels: 247 us -> 199 us  [on_device(): pl.pallas_call(relay_kernel, out_shape=jax.ShapeDtypeStruct((batches, row...]
where the time goes in v2:
time: 205 us; the launch traced here: 204 us
  Pallas kernels  199 us (97%)
  other arithmetic  2.8 us (1%)
  local copies, waits for them, and re-layouts  2.23 us (1%)
    pallas_call x1, Pallas kernels, on_device(): pl.pallas_call(relay_kernel, out_shape=jax.ShapeDtypeStruct((batches, row...  199 us

profile of v2, /device:TPU:97, one launch (start us, length us, event | category | flops | bytes accessed | tf_op | source)
XLA Modules:
  0.0 204.2 jit_solution(10334922297550507388)
XLA Ops:
  0.0 0.7 convert_element_type.6
  0.7 1.4 maximum_select_fusion.meta
  2.1 0.7 reduce
  2.8 0.6 broadcast_in_dim.26.gain
  3.4 199.2 %shard_map.64 = bf16[2,64,768]{2,1,0:T(8,128)(2,1)} custom-call(bf16[2,64,768]{2,1,0:T(8,128)(2,1)} %inp.1, f32[8,128]{1,0:T(8,128)} %maximum_select_fusion.meta, f32[8,768]{1,0:T(8,128)} %broadcast_in_dim.26.gain, bf16[3072,2048]{1,0:T(8,128)(2,1)} %bitcast.13, bf16[2048,3072]{1,0:T(8,128)(2,1)} %bitcast.14), custom_call_target="tpu_custom_call" | custom-call | tf_op jit(solution)/shard_map/pallas_call | solution.py:342
  202.6 1.6 copy.8
  (1 shorter events, 0.0 us)

commit v3 on v2

--- a/solution.py
+++ b/solution.py
@@ -15,8 +15,8 @@
 
 
 def relay_kernel(
-    inp, meta, gain, up_hbm, down_hbm, out,
-    wup, wdn, xbuf, obuf, pbuf, r2, r3, res, xg, acc, squares, hid, dmat, pmat, gslot, mbuf, gbuf, chosen,
+    inp, choice, gate_in, gain, up_hbm, down_hbm, out,
+    meta, wup, wdn, xbuf, obuf, pbuf, r2, r3, res, xg, acc, squares, hid, dmat, pmat, gslot, mbuf, gbuf, chosen,
     w_sem, m_send, m_recv, n_send, n_recv, z_send, z_recv,
     gf_recv, gg_recv, gp_recv, f_send, g_send, sp_recv, s2_recv, s3_recv, s_send,
 ):
@@ -66,6 +66,11 @@
     down_copy = pltpu.make_async_copy(down_hbm, wdn, w_sem.at[1])
     up_copy.start()
 
+    both = jnp.concatenate([choice[...].astype(F32), gate_in[...]], axis=0)
+    both = jnp.concatenate([both, both], axis=1)
+    lane = lax.broadcasted_iota(jnp.int32, both.shape, 1)
+    meta[...] = jnp.where(lane // rows == lax.rem(y, 2), both, 0.0)
+
     barrier = pltpu.get_barrier_semaphore()
     for step in range(1, 8):
         pl.semaphore_signal(barrier, inc=1, device_id={"expert": lax.rem(e + step, 8)}, device_id_type=MESH)
@@ -107,7 +112,7 @@
 
         def spread(number):
             ref = xbuf.at[base + place(g, order[number])]
-            for kind, dg in enumerate((1, -1, 2)):
+            for kind, dg in ((2, 2), (0, 1), (1, -1)):
                 send(ref, ref, g_send.at[m], gg_recv.at[m, number, kind], device(0, dg))
             to_partner(ref, number, 0)
 
@@ -123,6 +128,8 @@
                 arrive(own, z_recv.at[m, h])
                 for kind, df in ((2, 2), (0, 1), (1, -1)):
                     send(own, own, f_send.at[m], gf_recv.at[m, kind, h], device(df, 0))
+
+        def leave():
             arrive(xbuf.at[pl.ds(0, 3)], f_send.at[m])
             spread(0)
 
@@ -132,7 +139,7 @@
                     arrive(xbuf.at[base + place(g, fi), part(h)], gf_recv.at[m, number - 1, h])
                 spread(number)
 
-        return start, turn, pass_on
+        return start, leave, turn, pass_on
 
     def set_up_routing():
         for step in range(7):
@@ -174,7 +181,7 @@
             square = jnp.sum(picked * picked, axis=1, keepdims=True)
             mine = pl.ds(p * slots, slots)
             squares[mine] = square if number == 0 else squares[mine] + square
-            xg[mine] = (picked * gbuf[q, 0:1]).astype(BF16)
+            xg[mine] = (picked * gbuf[q]).astype(BF16)
         step = hidden // 2
         deep = pl.ds(pl.multiple_of(q * quarter, quarter), quarter)
         for i in range(2):
@@ -280,16 +287,19 @@
         set_up_routing()
         up_copy.wait()
 
-    def one_batch(m, carry):
-        start, turn, pass_on = gather_steps(m)
-        start()
+    steps = [gather_steps(m) for m in range(batches)]
+    for m in range(batches):
+        start, leave, turn, pass_on = steps[m]
+        if m == 0:
+            start()
+        leave()
         turn()
         pass_on(0)
-
-        @pl.when((s == 0) & (m == 0))
-        def _():
-            set_up_routing()
-            up_copy.wait()
+        if m == 0:
+            @pl.when(s == 0)
+            def _():
+                set_up_routing()
+                up_copy.wait()
 
         up(m, 0)
         pass_on(1)
@@ -299,19 +309,15 @@
         pass_on(3, (2,))
         up(m, 2)
         up(m, 3)
-
-        @pl.when(m == 0)
-        def _():
+        if m == 0:
             down_copy.wait()
-
         project(m)
         for number in range(RING - 1):
             second_ring(m, number)
+        if m + 1 < batches:
+            steps[m + 1][0]()
         finish(m)
         sent(m)
-        return carry
-
-    lax.fori_loop(0, batches, one_batch, 0)
 
     for step in range(7):
         arrive(meta, m_send.at[step])
@@ -327,14 +333,8 @@
 def on_device(inputs, norm_gain, up_weight, down_weight, routing, gates):
     batches, rows, quarter = inputs.shape
     width, hidden = up_weight.shape[2:]
-    lanes = 2 * rows
-    choice_rows = routing[0].astype(F32).transpose(0, 2, 1).reshape(2 * batches, rows)
-    gate_rows = gates[0].transpose(0, 2, 1).reshape(2 * batches, rows)
-    both = jnp.concatenate([choice_rows, gate_rows], axis=0)
-    place = lax.rem(lax.axis_index("expert") // 2, 2)
-    filled = jnp.concatenate([both, both], axis=1)
-    meta = jnp.where(jnp.arange(lanes)[None, :] // rows == place, filled, 0.0)
-    gain = jnp.broadcast_to(norm_gain, (8, quarter))
+    choice = routing[0].transpose(0, 2, 1).reshape(2 * batches, rows)
+    gate = gates[0].transpose(0, 2, 1).reshape(2 * batches, rows)
     slots = RING * CAP
     dma = pltpu.SemaphoreType.DMA
     vmem = pl.BlockSpec(memory_space=pltpu.VMEM)
@@ -342,9 +342,10 @@
     result = pl.pallas_call(
         relay_kernel,
         out_shape=jax.ShapeDtypeStruct((batches, rows, quarter), BF16),
-        in_specs=[vmem, vmem, vmem, hbm, hbm],
+        in_specs=[vmem, vmem, vmem, vmem, hbm, hbm],
         out_specs=vmem,
         scratch_shapes=[
+            pltpu.VMEM((8, 2 * rows), F32),
             pltpu.VMEM((width, hidden), BF16),
             pltpu.VMEM((hidden, width), BF16),
             pltpu.VMEM((batches * 2 * 16, rows, quarter), BF16),
@@ -360,8 +361,8 @@
             pltpu.VMEM((batches, 2, slots, RING * rows), BF16),
             pltpu.VMEM((batches, 2, RING * rows, slots), BF16),
             pltpu.VMEM((batches, 2 * slots, 1), F32),
-            pltpu.VMEM((8, 8, lanes), F32),
-            pltpu.VMEM((RING, 8, quarter), F32),
+            pltpu.VMEM((8, 8, 2 * rows), F32),
+            pltpu.VMEM((RING, 1, quarter), F32),
             pltpu.VMEM((16, RING * rows), BF16),
             dma((2,)),
             dma((8,)),
@@ -383,7 +384,7 @@
         compiler_params=pltpu.CompilerParams(
             collective_id=0, has_side_effects=True, vmem_limit_bytes=67043328
         ),
-    )(inputs, meta, gain, up_weight.reshape(width, hidden), down_weight.reshape(hidden, width))
+    )(inputs, choice, gate, norm_gain, up_weight.reshape(width, hidden), down_weight.reshape(hidden, width))
     return result[None]
 
 

time: 205 us -> 199 us (0.971)
  other arithmetic: 2.8 us -> 0 us
    pallas_call x1, Pallas kernels: 199 us -> 197 us  [on_device(): pl.pallas_call(relay_kernel, out_shape=jax.ShapeDtypeStruct((batches, row...]
where the time goes in v3:
time: 199 us
  Pallas kernels  197 us (99%)
    pallas_call x1, Pallas kernels, on_device(): pl.pallas_call(relay_kernel, out_shape=jax.ShapeDtypeStruct((batches, row...  197 us

profile of v3, /device:TPU:97, one launch (start us, length us, event | category | flops | bytes accessed | tf_op | source)
XLA Modules:
  0.0 198.5 jit_solution(17386073326142526641)
XLA Ops:
  0.0 196.9 %shard_map.64 = bf16[2,64,768]{2,1,0:T(8,128)(2,1)} custom-call(bf16[2,64,768]{2,1,0:T(8,128)(2,1)} %inp.1, s32[4,64]{1,0:T(4,128)} %bitcast.16, f32[4,64]{1,0:T(4,128)} %bitcast.17, f32[1,768]{1,0:T(1,128)} %gain.1, bf16[3072,2048]{1,0:T(8,128)(2,1)} %bitcast.13, bf16[2048,3072]{1,0:T(8,128)(2,1)} %bitcast.14), custom_call_target="tpu_custom_call" | custom-call | tf_op jit(solution)/shard_map/pallas_call | solution.py:342
  196.9 1.6 copy.8

commit v4 on v3

--- a/solution.py
+++ b/solution.py
@@ -66,10 +66,12 @@
     down_copy = pltpu.make_async_copy(down_hbm, wdn, w_sem.at[1])
     up_copy.start()
 
-    both = jnp.concatenate([choice[...].astype(F32), gate_in[...]], axis=0)
-    both = jnp.concatenate([both, both], axis=1)
-    lane = lax.broadcasted_iota(jnp.int32, both.shape, 1)
-    meta[...] = jnp.where(lane // rows == lax.rem(y, 2), both, 0.0)
+    @pl.when(s == 0)
+    def _():
+        for m in range(batches):
+            for h in range(2):
+                here = xbuf.at[(m * 2 + c) * 16 + place(g, f), part(h)]
+                pltpu.make_async_copy(inp.at[m, part(h)], here, z_recv.at[m, h]).start()
 
     barrier = pltpu.get_barrier_semaphore()
     for step in range(1, 8):
@@ -78,15 +80,14 @@
         pl.semaphore_signal(barrier, inc=1, device_id={"tensor": lax.rem(t + step, RING)}, device_id_type=MESH)
     pl.semaphore_signal(barrier, inc=1, device_id=above, device_id_type=MESH)
     pl.semaphore_signal(barrier, inc=1, device_id=below, device_id_type=MESH)
+
+    both = jnp.concatenate([choice[...].astype(F32), gate_in[...]], axis=0)
+    both = jnp.concatenate([both, both], axis=1)
+    lane = lax.broadcasted_iota(jnp.int32, both.shape, 1)
+    meta[...] = jnp.where(lane // rows == lax.rem(y, 2), both, 0.0)
+
     pl.semaphore_wait(barrier, 12)
     down_copy.start()
-
-    @pl.when(s == 0)
-    def _():
-        for m in range(batches):
-            for h in range(2):
-                here = xbuf.at[(m * 2 + c) * 16 + place(g, f), part(h)]
-                pltpu.make_async_copy(inp.at[m, part(h)], here, z_recv.at[m, h]).start()
 
     for step in range(1, 8):
         send(meta, mbuf.at[e], m_send.at[step - 1], m_recv.at[step - 1], {"expert": lax.rem(e + step, 8)})
@@ -182,18 +183,15 @@
             mine = pl.ds(p * slots, slots)
             squares[mine] = square if number == 0 else squares[mine] + square
             xg[mine] = (picked * gbuf[q]).astype(BF16)
-        step = hidden // 2
         deep = pl.ds(pl.multiple_of(q * quarter, quarter), quarter)
-        for i in range(2):
-            cols = pl.ds(i * step, step)
-            v = jnp.dot(xg[...], wup[deep, cols], preferred_element_type=F32)
-            if number > 0:
-                v = v + acc[:, cols]
-            if number < RING - 1:
-                acc[:, cols] = v
-            else:
-                v = v * lax.rsqrt(squares[...] / width + 1e-05)
-                hid[:, cols] = (v / (1.0 + jnp.exp(-v)) * gslot[m]).astype(BF16)
+        v = jnp.dot(xg[...], wup[deep, :], preferred_element_type=F32)
+        if number > 0:
+            v = v + acc[...]
+        if number < RING - 1:
+            acc[...] = v
+        else:
+            v = v * lax.rsqrt(squares[...] / width + 1e-05)
+            hid[...] = (v / (1.0 + jnp.exp(-v)) * gslot[m]).astype(BF16)
 
     def chunk(number):
         return mod4(t + (2, -1, 1, 0)[number])

time: 199 us -> 198 us (level)
  no operation moved by 1% of the time
where the time goes in v4:
time: 198 us
  Pallas kernels  196 us (99%)
    pallas_call x1, Pallas kernels, on_device(): pl.pallas_call(relay_kernel, out_shape=jax.ShapeDtypeStruct((batches, row...  196 us

profile of v4, /device:TPU:97, one launch (start us, length us, event | category | flops | bytes accessed | tf_op | source)
XLA Modules:
  0.0 197.9 jit_solution(8214090543641603802)
XLA Ops:
  0.0 196.2 %shard_map.64 = bf16[2,64,768]{2,1,0:T(8,128)(2,1)} custom-call(bf16[2,64,768]{2,1,0:T(8,128)(2,1)} %inp.1, s32[4,64]{1,0:T(4,128)} %bitcast.16, f32[4,64]{1,0:T(4,128)} %bitcast.17, f32[1,768]{1,0:T(1,128)} %gain.1, bf16[3072,2048]{1,0:T(8,128)(2,1)} %bitcast.13, bf16[2048,3072]{1,0:T(8,128)(2,1)} %bitcast.14), custom_call_target="tpu_custom_call" | custom-call | tf_op jit(solution)/shard_map/pallas_call | solution.py:340
  196.2 1.6 copy.8
